TPU v7x, 512 devices: a whole 4x4x16 slice. The times are simulated.
512 devices in a mesh: section: 4 (over x), ctx: 64 (over y_lo, z, core), tp: 2 (over y_hi).
Axes of the slice: x: 4, y: 4 (y_hi: 2, y_lo: 2; y = y_hi * 2 + y_lo), z: 16, core: 2. Of those that a mesh axis runs over, the one named last changes fastest.
Arguments:
- video_feats: bfloat16 [8192, 1024], P('ctx', ('section', 'tp')), may hold values from -512 to 512
- ir_feats: bfloat16 [2048, 768], P('ctx', ('section', 'tp')), may hold values from -512 to 512
- video_adapter: bfloat16 [1024, 8, 768], P(('section', 'tp')), may hold values from -0.1875 to 0.1875
- ir_adapter: bfloat16 [768, 8, 768], P(('section', 'tp')), may hold values from -0.21875 to 0.21875
- text_query: bfloat16 [6144, 4096], P('ctx', ('section', 'tp')), may hold values from -4.5 to 4.5
- text_key: bfloat16 [6144, 1024], P('ctx', ('section', 'tp')), may hold values from -4.5 to 4.5
- text_value: bfloat16 [6144, 1024], P('ctx', ('section', 'tp')), may hold values from -6 to 6
- frame_live_counts: int32 [64, 2], replicated, may hold values from 1 to 128, as said below
- block_mask: int32 [64, 64], replicated, may hold values from 0 to 1, as said below
Outputs:
- attended: bfloat16 [16384, 4096], P('ctx', ('section', 'tp'))
Inputs may be any that keep to these rules, and one draw needn't show every extreme that they name: frame_live_counts[f][0] of the 128 video slots and frame_live_counts[f][1] of the 32 IR slots of frame f are live, the first ones of each; some frame has all of its slots live. block_mask[b][c] is 1 where c = b and 0 where c > b.
All inputs are finite; a program needn't handle non-finite values.
Results may differ from a plain program's by a relative error of at most 0.02.
Values may be sent and summed in bfloat16 or wider, within the bound.
A program may use at most 64 MiB of HBM per device.

v0:
```python
import jax
import jax.numpy as jnp
from jax import lax
from jax.sharding import PartitionSpec as P

HEAD_DIM = 128
D_VID = 1024
D_IR = 768
VTOK = 128
ITOK = 32
XTOK = 96
QPK = 4
GW = 768
BLK = 256


LN_EPSILON = 1e-05
NEG_LARGE = -1e30


def normalize(values, row_sums, squares, feature_count):
    center = row_sums / feature_count
    spread = squares / feature_count - center * center
    return ((values - center[:, None]) * lax.rsqrt(spread + LN_EPSILON)[:, None]).astype(
        jnp.bfloat16
    )


def shards(
    video_feats,
    ir_feats,
    video_adapter,
    ir_adapter,
    text_query,
    text_key,
    text_value,
    frame_live_counts,
    block_mask,
):
    video_count = video_feats.shape[0]
    frames_here = video_count // VTOK
    rows_here = frames_here * BLK
    query_width = QPK * HEAD_DIM
    video_values = video_feats.astype(jnp.float32)
    ir_values = ir_feats.astype(jnp.float32)
    moments = lax.psum(
        (
            jnp.sum(video_values, axis=1),
            jnp.sum(video_values * video_values, axis=1),
            jnp.sum(ir_values, axis=1),
            jnp.sum(ir_values * ir_values, axis=1),
        ),
        ("section", "tp"),
    )
    video_normed = normalize(video_values, moments[0], moments[1], D_VID)
    ir_normed = normalize(ir_values, moments[2], moments[3], D_IR)
    video_part = video_adapter
    ir_part = ir_adapter
    video_term = jnp.einsum(
        "rd,dgc->grc", video_normed, video_part, preferred_element_type=jnp.float32
    )
    ir_term = jnp.einsum("rd,dgc->grc", ir_normed, ir_part, preferred_element_type=jnp.float32)
    projected = lax.psum_scatter(
        jnp.concatenate([video_term, ir_term], axis=1).astype(jnp.bfloat16),
        ("section", "tp"),
        scatter_dimension=0,
        tiled=True,
    ).astype(jnp.float32)[0]
    joint_rows = projected.astype(jnp.bfloat16)
    video_part = joint_rows[:video_count].reshape(frames_here, VTOK, GW)
    ir_part = joint_rows[video_count:].reshape(frames_here, ITOK, GW)
    query_rows = jnp.concatenate(
        [
            video_part[:, :, :query_width],
            ir_part[:, :, :query_width],
            text_query.reshape(frames_here, XTOK, query_width),
        ],
        axis=1,
    ).reshape(rows_here * QPK, HEAD_DIM)
    key_rows = jnp.concatenate(
        [
            video_part[:, :, query_width : query_width + HEAD_DIM],
            ir_part[:, :, query_width : query_width + HEAD_DIM],
            text_key.reshape(frames_here, XTOK, HEAD_DIM),
        ],
        axis=1,
    ).reshape(rows_here, HEAD_DIM)
    value_rows = jnp.concatenate(
        [
            video_part[:, :, query_width + HEAD_DIM :],
            ir_part[:, :, query_width + HEAD_DIM :],
            text_value.reshape(frames_here, XTOK, HEAD_DIM),
        ],
        axis=1,
    ).reshape(rows_here, HEAD_DIM)
    ctx_position = lax.axis_index("ctx")
    query_position = ctx_position * rows_here + jnp.arange(rows_here, dtype=jnp.int32)
    own_mask = lax.dynamic_slice_in_dim(block_mask, ctx_position * frames_here, frames_here, 0)
    frame_ids = jnp.arange(block_mask.shape[1], dtype=jnp.int32)
    scale = HEAD_DIM ** (-0.5)
    start_state = (
        jnp.full((rows_here * QPK,), NEG_LARGE, jnp.float32),
        jnp.zeros((rows_here * QPK,), jnp.float32),
        jnp.zeros((rows_here * QPK, HEAD_DIM), jnp.float32),
    )
    state_now = start_state
    key_piece = lax.all_gather(key_rows, "ctx", axis=0, tiled=True)
    value_piece = lax.all_gather(value_rows, "ctx", axis=0, tiled=True)
    piece_rows = key_piece.shape[0]
    block_width = BLK

    def one_block(block_index, state_now):
        offset = block_index * block_width
        key_block = lax.dynamic_slice_in_dim(key_piece, offset, block_width, 0)
        value_block = lax.dynamic_slice_in_dim(value_piece, offset, block_width, 0)
        key_position = offset + jnp.arange(block_width, dtype=jnp.int32)
        key_frame_ids = key_position // BLK
        key_slot = key_position % BLK
        frame_hit = key_frame_ids[:, None] == frame_ids[None, :]
        video_live = jnp.sum(jnp.where(frame_hit, frame_live_counts[:, 0][None, :], 0), axis=1)
        ir_live = jnp.sum(jnp.where(frame_hit, frame_live_counts[:, 1][None, :], 0), axis=1)
        key_live = jnp.where(
            key_slot < VTOK,
            key_slot < video_live,
            jnp.where(key_slot < VTOK + ITOK, key_slot - VTOK < ir_live, True),
        )
        frame_open = jnp.sum(jnp.where(frame_hit[None, :, :], own_mask[:, None, :], 0), axis=2) > 0
        row_open = jnp.repeat(frame_open, BLK, axis=0)
        permitted_mask = (
            row_open & (key_position[None, :] <= query_position[:, None]) & key_live[None, :]
        )

        def update(state_now):
            row_top, row_sums, weighted = state_now
            open_rep = jnp.repeat(permitted_mask, QPK, axis=0)
            scores = jnp.dot(query_rows, key_block.T, preferred_element_type=jnp.float32) * scale
            new_top = jnp.maximum(row_top, jnp.max(jnp.where(open_rep, scores, NEG_LARGE), axis=1))
            weights = jnp.where(open_rep, jnp.exp(scores - new_top[:, None]), 0.0)
            factor = jnp.exp(row_top - new_top)
            row_sums = row_sums * factor + jnp.sum(weights, axis=1)
            weighted = weighted * factor[:, None] + jnp.dot(
                weights.astype(jnp.bfloat16), value_block, preferred_element_type=jnp.float32
            )
            return (new_top, row_sums, weighted)

        return lax.cond(jnp.any(permitted_mask), update, lambda kept: kept, state_now)

    row_top, row_sums, weighted = lax.fori_loop(0, piece_rows // block_width, one_block, state_now)
    return (weighted / row_sums[:, None]).astype(jnp.bfloat16).reshape(rows_here, query_width)


def solution(mesh):
    return jax.shard_map(
        shards,
        mesh=mesh,
        in_specs=(
            P("ctx", ("section", "tp")),
            P("ctx", ("section", "tp")),
            P(("section", "tp"), None, None),
            P(("section", "tp"), None, None),
            P("ctx", ("section", "tp")),
            P("ctx", ("section", "tp")),
            P("ctx", ("section", "tp")),
            P(),
            P(),
        ),
        out_specs=P("ctx", ("section", "tp")),
        check_vma=False,
    )
```

profile of v0, /device:TPU:493, one launch (start us, length us, event | category | flops | bytes accessed | tf_op | source)
XLA Modules:
  0.0 623.1 jit_solution(4839542533983586553)
XLA Ops:
  8.3 15.6 %all-reduce = (f32[32]{0:T(128)S(1)}, f32[32]{0:T(128)S(1)}, f32[128]{0:T(128)S(1)}, f32[128]{0:T(128)S(1)}) all-reduce(f32[32]{0:T(128)S(1)} %get-tuple-element.458, f32[32]{0:T(128)S(1)} %get-tuple-element.457, f32[128]{0:T(128)S(1)} %get-tuple-element.456, ...), channel_id=1, replica_groups=mesh['section'=4,'ctx'=64,'tp'=2] {'section','tp'}, use_global_device_ids=true, to_apply=%region_7.0 | all-reduce | flops 320 | bytes 2560 | tf_op jit(solution)/shard_map/psum | solution.py:46
  23.9 1.7 fusion.24
  25.6 1.4 fusion.21
  27.1 1.4 pad_maximum_fusion
  28.6 90.8 %reduce-scatter.2.cloned.1.call-done = bf16[1,160,768]{2,1,0:T(8,128)(2,1)} async-done(((bf16[8,160,768]{2,1,0:T(8,128)(2,1)}), bf16[1,160,768]{2,1,0:T(8,128)(2,1)}) %reduce-scatter.2.cloned.1.call-update) | async-done | bytes 245776 | tf_op jit(solution)/shard_map/reduce_scatter | solution.py:63
  123.4 122.3 %all-gather.7.cloned.1.call-done = bf16[1,16384,128]{2,1,0:T(8,128)(2,1)} async-done(((bf16[1,256,128]{2,1,0:T(8,128)(2,1)}), bf16[1,16384,128]{2,1,0:T(8,128)(2,1)}) %all-gather.7.cloned.1.call-update) | async-done | bytes 4194320 | tf_op jit(solution)/shard_map/all_gather | solution.py:108
  245.7 122.2 %all-gather.5.cloned.1.call-done = bf16[1,16384,128]{2,1,0:T(8,128)(2,1)} async-done(((bf16[1,256,128]{2,1,0:T(8,128)(2,1)}), bf16[1,16384,128]{2,1,0:T(8,128)(2,1)}) %all-gather.5.cloned.1.call-update) | async-done | bytes 4194320 | tf_op jit(solution)/shard_map/all_gather | solution.py:107
  368.0 247.5 %while.21 = (s32[]{:T(128)}, f32[1024]{0:T(1024)S(1)}, f32[1024]{0:T(1024)S(1)}, f32[1024,128]{1,0:T(8,128)S(1)}, s32[1,64]{1,0:T(1,128)S(1)}, /*index=5*/s32[64...) while((s32[]{:T(128)}, f32[1024]{0:T(1024)S(1)}, ...), condition=%wide.region_18.19_spmd.clone.clone, body=%wide.region_9.18_spmd.clone.clone.sunk | while | flops 137243136 | bytes 6897717 | solution.py:148
  369.6 3.7 conditional.4
  371.9 1.4 convolution_add_fusion
  374.9 3.7 conditional.4
  381.8 3.7 conditional.4
  388.7 3.7 conditional.4
  394.1 3.7 conditional.4
  399.4 3.7 conditional.4
  404.7 3.7 conditional.4
  410.0 3.7 conditional.4
  415.3 3.7 conditional.4
  422.2 3.7 conditional.4
  427.5 3.7 conditional.4
  437.7 3.7 conditional.4
  446.2 3.7 conditional.4
  451.5 3.7 conditional.4
  456.9 3.7 conditional.4
  463.8 3.7 conditional.4
  469.1 3.7 conditional.4
  479.2 3.7 conditional.4
  484.6 3.7 conditional.4
  489.9 3.7 conditional.4
  495.2 3.7 conditional.4
  503.7 3.7 conditional.4
  509.0 3.7 conditional.4
  514.3 3.7 conditional.4
  521.3 3.7 conditional.4
  528.2 3.7 conditional.4
  533.5 3.7 conditional.4
  540.4 3.7 conditional.4
  549.0 3.7 conditional.4
  554.3 3.7 conditional.4
  559.6 3.7 conditional.4
  569.7 3.7 conditional.4
  578.3 3.7 conditional.4
  583.6 3.7 conditional.4
  588.9 3.7 conditional.4
  594.2 3.7 conditional.4
  599.5 3.7 conditional.4
  606.5 3.7 conditional.4
  611.8 3.7 conditional.4
  (919 shorter events, 209.5 us)
Async XLA Ops:
  6.5 19.1 %copy-start = (bf16[128,8,768]{2,1,0:T(8,128)(2,1)S(1)}, bf16[128,8,768]{2,1,0:T(8,128)(2,1)}, u32[]{:S(2)}) copy-start(bf16[128,8,768]{2,1,0:T(8,128)(2,1)} %param.15) | copy-start | bytes 4718596
  6.5 112.8 %reduce-scatter.2.cloned.1.call-start = ((), (), s32[]{:S(2)}) async-start(), calls=%async_computation.1 | async-start | bytes 2211840 | tf_op jit(solution)/shard_map/reduce_scatter | solution.py:63
  28.5 91.7 %copy-start.3 = (bf16[96,128]{1,0:T(8,128)(2,1)S(1)}, bf16[96,128]{1,0:T(8,128)(2,1)}, u32[]{:S(2)}) copy-start(bf16[96,128]{1,0:T(8,128)(2,1)} %param.19) | copy-start | bytes 73732
  28.5 92.4 %copy-start.4 = (bf16[96,128]{1,0:T(8,128)(2,1)S(1)}, bf16[96,128]{1,0:T(8,128)(2,1)}, u32[]{:S(2)}) copy-start(bf16[96,128]{1,0:T(8,128)(2,1)} %param.18) | copy-start | bytes 73732
  28.5 94.7 %copy-start.1 = (bf16[96,512]{1,0:T(8,128)(2,1)S(1)}, bf16[96,512]{1,0:T(8,128)(2,1)}, u32[]{:S(2)}) copy-start(bf16[96,512]{1,0:T(8,128)(2,1)} %param.17) | copy-start | bytes 294916
  28.5 339.5 %copy-start.2 = (s32[64,2]{0,1:T(2,128)S(1)}, s32[64,2]{0,1:T(2,128)}, u32[]{:S(2)}) copy-start(s32[64,2]{0,1:T(2,128)} %param.20) | copy-start | bytes 1540
  28.5 217.2 %all-gather.7.cloned.1.call-start = ((), (), s32[]{:S(2)}) async-start(), calls=%async_computation.3 | async-start | bytes 4259840 | tf_op jit(solution)/shard_map/all_gather | solution.py:108
  120.8 247.1 %all-gather.5.cloned.1.call-start = ((), (), s32[]{:S(2)}) async-start(), calls=%async_computation.2 | async-start | bytes 4259840 | tf_op jit(solution)/shard_map/all_gather | solution.py:107
Sparse Core Ops, SparseCore 0:
  28.6 90.6 reduce-scatter.1
  121.5 124.1 all-gather.6
  247.9 119.9 all-gather.4
where the time goes:
time: 628 us; the launch traced here: 623 us
  waiting for transfers between devices  335 us (53%)
  matrix products  102 us (16%)
  other arithmetic  77 us (12%)
  loops' own time  43.9 us (7%)
  local copies, waits for them, and re-layouts  35.6 us (6%)
  blocking collectives  15.6 us (2%)
  between operations  13.2 us (2%)
    all_gather x1, waiting for transfers between devices, shards(): value_piece = lax.all_gather(value_rows, 'ctx', axis=0, tiled=True)  122 us
    all_gather x1, waiting for transfers between devices, shards(): key_piece = lax.all_gather(key_rows, 'ctx', axis=0, tiled=True)  122 us
    reduce_scatter x1, waiting for transfers between devices, shards(): lax.psum_scatter(jnp.concatenate([video_term, ir_term], axis=1).astype(jn...  90.8 us
    dot_general x39, matrix products, update(): jnp.dot(weights.astype(jnp.bfloat16), value_block, preferred_element_type...  53.2 us
    reduce_or x64, other arithmetic, one_block(): jnp.any(permitted_mask)  47.1 us
    dot_general x39, matrix products, update(): jnp.dot(query_rows, key_block.T, preferred_element_type=jnp.float32) * scale  46.1 us
    another operation x1, loops' own time, shards(): lax.fori_loop(0, piece_rows // block_width, one_block, state_now)  40.4 us
    reshape x78, local copies, waits for them, and re-layouts, update(): open_rep = jnp.repeat(permitted_mask, QPK, axis=0)  22.3 us
  transfers between devices with their start and end apart: 3, of which 3 were waited for; matrix products, arithmetic and copies ran while one was open for 0% of the time, Pallas kernels for 0%

commit v1 on v0

v1 whole, which is shorter than its diff:
```python
import functools

import jax
import jax.numpy as jnp
from jax import lax
from jax.experimental import pallas as pl
from jax.experimental.pallas import tpu as pltpu
from jax.sharding import PartitionSpec as P

HEAD_DIM = 128
D_VID = 1024
D_IR = 768
VTOK = 128
ITOK = 32
ENC = VTOK + ITOK
XTOK = 96
QPK = 4
QW = QPK * HEAD_DIM
GW = 768
KVW = 2 * HEAD_DIM
BLK = 256
PAIR = 2 * BLK

LN_EPSILON = 1e-05
NEG_LARGE = -1e30
LOG2E = 1.4426950408889634
MESH = pl.DeviceIdType.MESH

PIECES = ((ENC, XTOK), (0, ENC // 2), (ENC // 2, ENC // 2))
TEXT, FIRST, SECOND = 0, 1, 2
PROJ_TICK = 4
STREAMS = ((TEXT, 0), (FIRST, PROJ_TICK), (SECOND, PROJ_TICK), (SECOND, PROJ_TICK + 1))
LAG = 2


def kernel(
    n_section,
    n_ctx,
    n_tp,
    vf_ref,
    if_ref,
    wv_ref,
    wi_ref,
    tq_ref,
    tk_ref,
    tv_ref,
    counts_ref,
    mask_ref,
    out_ref,
    kv,
    bias,
    xv,
    xi,
    wvb,
    wib,
    qa,
    top,
    acc,
    kv_recv,
    z_send,
    core_send,
    y_send,
    yc_send,
    x_recv,
    x_send,
    w_recv,
    w_send,
    w_fwd,
    local_sem,
):
    section = lax.axis_index("section")
    ctx = lax.axis_index("ctx")
    tp = lax.axis_index("tp")
    n_z = n_ctx // 4
    half = n_z // 2
    row = ctx // (2 * n_z)
    z = (ctx // 2) % n_z
    core = ctx % 2
    shard = section * n_tp + tp
    n_shard = n_section * n_tp

    def frame_at(r, zz, k):
        return r * (2 * n_z) + zz * 2 + k

    core_peer = {"ctx": frame_at(row, z, 1 - core)}
    y_peer = {"ctx": frame_at(1 - row, z, core)}
    z_peer = (
        {"ctx": frame_at(row, (z + 1) % n_z, core)},
        {"ctx": frame_at(row, (z + n_z - 1) % n_z, core)},
    )
    others = [(a, b) for a in range(n_section) for b in range(n_tp) if (a, b) != (0, 0)]

    def feature_peer(a, b):
        return {"section": (section + a) % n_section, "tp": (tp + b) % n_tp}

    def weight_peer(a, b):
        peer = feature_peer(a, b)
        if b:
            peer["ctx"] = frame_at(1 - row, z, core)
        return peer

    barrier = pltpu.get_barrier_semaphore()
    greeted = [core_peer, y_peer, z_peer[0], z_peer[1]]
    greeted += [feature_peer(a, b) for a, b in others]
    greeted += [weight_peer(a, b) for a, b in others if b]
    for peer in greeted:
        pl.semaphore_signal(barrier, inc=1, device_id=peer, device_id_type=MESH)

    own_rows = pl.multiple_of(ctx * BLK, BLK)
    own_group = shard
    v_half, i_half = D_VID // n_shard // 2, D_IR // n_shard // 2
    v_rows, i_rows = 2 * v_half, 2 * i_half
    locals_ = [
        pltpu.make_async_copy(tk_ref, kv.at[pl.ds(own_rows + ENC, XTOK), pl.ds(0, HEAD_DIM)], local_sem.at[0]),
        pltpu.make_async_copy(tv_ref, kv.at[pl.ds(own_rows + ENC, XTOK), pl.ds(HEAD_DIM, HEAD_DIM)], local_sem.at[1]),
        pltpu.make_async_copy(vf_ref, xv.at[:, pl.ds(pl.multiple_of(shard * 128, 128), 128)], local_sem.at[2]),
        pltpu.make_async_copy(if_ref, xi.at[shard], local_sem.at[3]),
        pltpu.make_async_copy(wv_ref.at[own_group], wvb.at[pl.ds(pl.multiple_of(shard * v_rows, v_rows), v_rows)], local_sem.at[4]),
        pltpu.make_async_copy(wi_ref.at[own_group], wib.at[shard], local_sem.at[5]),
    ]
    for copy in locals_:
        copy.start()

    def remote(src, dst, send_sem, recv_sem, peer):
        return pltpu.make_async_remote_copy(
            src_ref=src, dst_ref=dst, send_sem=send_sem, recv_sem=recv_sem, device_id=peer, device_id_type=MESH
        )

    def feature_sends(n):
        peer = feature_peer(*others[n])
        columns = pl.ds(pl.multiple_of(shard * 128, 128), 128)
        return [
            remote(vf_ref, xv.at[:, columns], x_send.at[0, n], x_recv.at[0, shard], peer),
            remote(if_ref, xi.at[shard], x_send.at[1, n], x_recv.at[1, shard], peer),
        ]

    parts = (pl.ds(QW, KVW), pl.ds(0, QW))

    def weight_places(src_shard, k, part):
        v_at = pl.ds(pl.multiple_of(src_shard * v_rows + k * v_half, v_half), v_half)
        i_at = pl.ds(pl.multiple_of(k * i_half, i_half), i_half)
        return wvb.at[v_at, parts[part]], wib.at[src_shard, i_at, parts[part]]

    def weight_sends(n, part):
        a, b = others[n]
        group = ((section + a) % n_section) * n_tp + (tp + b) % n_tp
        v_dst, i_dst = weight_places(shard, core, part)
        v_at = pl.ds(pl.multiple_of(core * v_half, v_half), v_half)
        i_at = pl.ds(pl.multiple_of(core * i_half, i_half), i_half)
        peer = weight_peer(a, b)
        return [
            remote(wv_ref.at[group, v_at, parts[part]], v_dst, w_send.at[0, part, n], w_recv.at[0, part, 0, shard], peer),
            remote(wi_ref.at[group, i_at, parts[part]], i_dst, w_send.at[1, part, n], w_recv.at[1, part, 0, shard], peer),
        ]

    def weight_forwards(n, part):
        a, b = others[n]
        src_shard = ((section + a) % n_section) * n_tp + (tp + b) % n_tp
        places = weight_places(src_shard, core, part)
        return [
            remote(place, place, w_fwd.at[i, part, n], w_recv.at[i, part, 1, src_shard], core_peer)
            for i, place in enumerate(places)
        ]

    def weight_arrivals(n, part, hop):
        a, b = others[n]
        src_shard = ((section + a) % n_section) * n_tp + (tp + b) % n_tp
        places = weight_places(src_shard, core if hop == 0 else 1 - core, part)
        return [
            remote(place, place, w_fwd.at[i, part, n], w_recv.at[i, part, hop, src_shard], core_peer)
            for i, place in enumerate(places)
        ]

    def piece_at(frame, piece):
        first, count = PIECES[piece]
        return kv.at[pl.ds(pl.multiple_of(frame * BLK + first, 16), count)]

    def arrived(frame, piece):
        place = piece_at(frame, piece)
        remote(place, place, z_send.at[0, 0, 0], kv_recv.at[frame, piece], core_peer).wait_recv()

    def send(frame, piece, sem, peer):
        place = piece_at(frame, piece)
        return remote(place, place, sem, kv_recv.at[frame, piece], peer)

    def reach(way):
        return half - core if way == 0 else half - 1 + core

    def z_of(way, distance):
        return (z + n_z - distance) % n_z if way == 0 else (z + distance) % n_z

    def act(copy, start):
        if start:
            copy.start()
        else:
            copy.wait_send()

    def line_step(tick, way, stream, start):
        piece, offset = STREAMS[stream]
        distance = tick - offset
        slot = tick % 2
        frame = frame_at(0 if stream == 3 else row, z_of(way, (distance + n_z) % n_z), core)
        active = (distance >= 0) & (distance <= reach(way))
        if stream == 3:
            active = active & (row == 1)

        @pl.when(active)
        def _():
            if start:
                if stream == 3 and way == 0:
                    arrived(frame, piece)
                else:
                    @pl.when(distance >= 1)
                    def _():
                        arrived(frame, piece)

            @pl.when(distance < reach(way))
            def _():
                act(send(frame, piece, z_send.at[way, stream, slot], z_peer[way]), start)

            if way == 0:
                act(send(frame, piece, core_send.at[way, stream, slot], core_peer), start)
            else:
                @pl.when(distance >= 1)
                def _():
                    act(send(frame, piece, core_send.at[way, stream, slot], core_peer), start)

            if stream in (0, 1):
                crosses = row == 0
                if way == 1:
                    crosses = crosses & (distance >= 1)
            elif stream == 2 and way == 0:
                crosses = (row == 0) & (distance == 0)
            else:
                crosses = None
            if crosses is not None:
                @pl.when(crosses)
                def _():
                    act(send(frame, piece, y_send.at[way, stream, slot], y_peer), start)

    def cross_step(tick, way, stream, start):
        piece, offset = STREAMS[stream]
        distance = tick - offset - 1
        slot = tick % 2
        frame = frame_at(0, z_of(way, (distance + n_z) % n_z), core)
        least = 0 if way == 0 else 1

        @pl.when((row == 1) & (distance >= least) & (distance <= reach(way)))
        def _():
            if start:
                arrived(frame, piece)
            act(send(frame, piece, yc_send.at[way, stream, slot], core_peer), start)

    def relay(tick, start=True):
        for stream in range(4):
            for way in range(2):
                line_step(tick, way, stream, start)
        for stream in range(2):
            for way in range(2):
                cross_step(tick, way, stream, start)

    def step(tick):
        relay(tick - 2, start=False)
        relay(tick)

    def attend(first_frame, diagonal):
        rows = pl.ds(pl.multiple_of(first_frame * BLK, PAIR), PAIR)
        keys = jnp.concatenate([kv[rows, :HEAD_DIM], bias[rows, :]], axis=1)
        values = jnp.concatenate([kv[rows, HEAD_DIM:], jnp.ones((PAIR, HEAD_DIM), jnp.bfloat16)], axis=1)
        for h in range(QPK):
            scores = lax.dot_general(
                qa[h], keys, (((1,), (1,)), ((), ())), preferred_element_type=jnp.float32
            )
            if diagonal:
                key_slot = lax.broadcasted_iota(jnp.int32, (BLK, PAIR), 1)
                query_slot = lax.broadcasted_iota(jnp.int32, (BLK, PAIR), 0) + core * BLK
                scores = jnp.where(key_slot <= query_slot, scores, NEG_LARGE)
            old = top[h]
            new = jnp.maximum(old, jnp.max(scores, axis=1, keepdims=True))
            top[h] = new
            weights = jnp.concatenate(
                [jnp.exp2(scores[:, i : i + HEAD_DIM] - new) for i in range(0, PAIR, HEAD_DIM)], axis=1
            ).astype(jnp.bfloat16)
            factor = jnp.exp2(old - new)
            acc[h] = acc[h] * jnp.concatenate([factor, factor], axis=1) + jnp.dot(
                weights, values, preferred_element_type=jnp.float32
            )

    def compute(distance):
        def item(n, _):
            way, r = n // 2, n % 2
            zz = jnp.where(way == 0, z + n_z - distance, z + distance) % n_z
            present = (r <= row) & (distance <= half) & ((way == 0) | ((distance >= 1) & (distance < half)))
            mine = (r == row) & (distance == 0)
            present = present & jnp.logical_not(mine)

            @pl.when(present)
            def _():
                for piece in range(3):
                    arrived(frame_at(r, zz, 1 - core), piece)

                @pl.when((r < row) | (zz < z))
                def _():
                    attend(frame_at(r, zz, 0), False)

            return 0

        lax.fori_loop(0, 4, item, 0)

    pl.semaphore_wait(barrier, len(greeted))
    locals_[0].wait()
    locals_[1].wait()
    for n in range(len(others)):
        for copy in feature_sends(n):
            copy.start()
    relay(0)
    for part in range(2):
        for n in range(len(others)):
            for copy in weight_sends(n, part):
                copy.start()

    def mask_frame(f, _):
        seen = mask_ref[ctx, f]
        video_live = counts_ref[f, 0] * seen
        ir_live = counts_ref[f, 1] * seen
        text_live = XTOK * seen
        base = pl.multiple_of(f * BLK, BLK)
        for first, count, live in ((0, VTOK, video_live), (VTOK, ITOK, ir_live), (ENC, XTOK, text_live)):
            slot = lax.broadcasted_iota(jnp.int32, (count, HEAD_DIM), 0)
            bias[pl.ds(base + first, count), :] = jnp.where(slot < live, 0.0, NEG_LARGE).astype(jnp.bfloat16)
        return 0

    lax.fori_loop(0, n_ctx, mask_frame, 0)

    for h in range(QPK):
        lane = lax.broadcasted_iota(jnp.int32, (BLK, HEAD_DIM), 1)
        qa[h, :, HEAD_DIM:] = jnp.where(lane == 0, 1.0, 0.0).astype(jnp.bfloat16)
        top[h] = jnp.full((BLK, HEAD_DIM), NEG_LARGE, jnp.float32)
        acc[h] = jnp.zeros((BLK, 2 * HEAD_DIM), jnp.float32)

    def early(tick, _):
        step(tick)
        return 0

    lax.fori_loop(1, PROJ_TICK, early, 0)

    for copy in locals_[2:]:
        copy.wait()
    for n in range(len(others)):
        a, b = others[n]
        src_shard = ((section + a) % n_section) * n_tp + (tp + b) % n_tp
        columns = pl.ds(pl.multiple_of(src_shard * 128, 128), 128)
        remote(xv.at[:, columns], xv.at[:, columns], x_send.at[0, n], x_recv.at[0, src_shard], core_peer).wait_recv()
        remote(xi.at[src_shard], xi.at[src_shard], x_send.at[1, n], x_recv.at[1, src_shard], core_peer).wait_recv()

    def norm_terms(total, squares, count):
        center = total / count
        spread = squares / count - center * center
        return center, lax.rsqrt(spread + LN_EPSILON)

    video = xv[...].astype(jnp.float32)
    center, gain = norm_terms(
        jnp.sum(video, axis=1, keepdims=True), jnp.sum(video * video, axis=1, keepdims=True), D_VID
    )
    xv[...] = ((video - center) * gain).astype(jnp.bfloat16)
    infra = [xi[n].astype(jnp.float32) for n in range(n_shard)]
    total = sum(jnp.sum(x, axis=1, keepdims=True) for x in infra)
    squares = sum(jnp.sum(x * x, axis=1, keepdims=True) for x in infra)
    center, gain = norm_terms(total, squares, D_IR)
    for n in range(n_shard):
        xi[n] = ((infra[n] - center) * gain).astype(jnp.bfloat16)

    def take_weights(part):
        for n in range(len(others)):
            for arrival, forward in zip(weight_arrivals(n, part, 0), weight_forwards(n, part)):
                arrival.wait_recv()
                forward.start()
        for n in range(len(others)):
            for arrival in weight_arrivals(n, part, 1):
                arrival.wait_recv()

    def project(columns):
        video_out = jnp.dot(xv[...], wvb[:, columns], preferred_element_type=jnp.float32)
        ir_out = sum(
            jnp.dot(xi[n], wib[n, :, columns], preferred_element_type=jnp.float32) for n in range(n_shard)
        )
        return video_out, ir_out

    take_weights(0)
    video_out, ir_out = project(slice(QW, GW))
    kv[pl.ds(own_rows, VTOK), :] = video_out.astype(jnp.bfloat16)
    kv[pl.ds(own_rows + VTOK, ITOK), :] = ir_out.astype(jnp.bfloat16)

    lax.fori_loop(PROJ_TICK, PROJ_TICK + 2 + LAG, early, 0)

    take_weights(1)
    scale = HEAD_DIM ** (-0.5) * LOG2E
    video_out, ir_out = project(slice(0, QW))
    for h in range(QPK):
        columns = slice(h * HEAD_DIM, (h + 1) * HEAD_DIM)
        qa[h, :VTOK, :HEAD_DIM] = (video_out[:, columns] * scale).astype(jnp.bfloat16)
        qa[h, VTOK:ENC, :HEAD_DIM] = (ir_out[:, columns] * scale).astype(jnp.bfloat16)
        qa[h, ENC:, :HEAD_DIM] = (tq_ref[:, columns].astype(jnp.float32) * scale).astype(jnp.bfloat16)

    for piece in range(3):
        arrived(frame_at(row, z, 1 - core), piece)
    attend(frame_at(row, z, 0), True)

    def late(tick, _):
        step(tick)
        compute(tick - PROJ_TICK - 2 - LAG)
        return 0

    last = half + PROJ_TICK + 3 + LAG
    lax.fori_loop(PROJ_TICK + 2 + LAG, last, late, 0)

    for h in range(QPK):
        out_ref[:, h * HEAD_DIM : (h + 1) * HEAD_DIM] = (
            acc[h, :, :HEAD_DIM] / acc[h, :, HEAD_DIM:]
        ).astype(jnp.bfloat16)

    relay(last - 2, start=False)
    relay(last - 1, start=False)
    for n in range(len(others)):
        for copy in feature_sends(n):
            copy.wait_send()
        for part in range(2):
            for copy in weight_sends(n, part) + weight_forwards(n, part):
                copy.wait_send()


def solution(mesh):
    n_section, n_ctx, n_tp = mesh.shape["section"], mesh.shape["ctx"], mesh.shape["tp"]
    n_shard = n_section * n_tp

    def shards(vf, irf, wv, wi, tq, tk, tv, counts, mask):
        anywhere = pl.BlockSpec(memory_space=pl.ANY)
        vmem = pl.BlockSpec(memory_space=pltpu.VMEM)
        smem = pl.BlockSpec(memory_space=pltpu.SMEM)
        dma = pltpu.SemaphoreType.DMA
        return pl.pallas_call(
            functools.partial(kernel, n_section, n_ctx, n_tp),
            out_shape=jax.ShapeDtypeStruct((BLK, QW), jnp.bfloat16),
            in_specs=[anywhere] * 4 + [vmem] + [anywhere] * 2 + [smem] * 2,
            out_specs=vmem,
            scratch_shapes=[
                pltpu.VMEM((n_ctx * BLK, KVW), jnp.bfloat16),
                pltpu.VMEM((n_ctx * BLK, HEAD_DIM), jnp.bfloat16),
                pltpu.VMEM((VTOK, D_VID), jnp.bfloat16),
                pltpu.VMEM((n_shard, ITOK, D_IR // n_shard), jnp.bfloat16),
                pltpu.VMEM((D_VID, GW), jnp.bfloat16),
                pltpu.VMEM((n_shard, D_IR // n_shard, GW), jnp.bfloat16),
                pltpu.VMEM((QPK, BLK, 2 * HEAD_DIM), jnp.bfloat16),
                pltpu.VMEM((QPK, BLK, HEAD_DIM), jnp.float32),
                pltpu.VMEM((QPK, BLK, 2 * HEAD_DIM), jnp.float32),
                dma((n_ctx, 3)),
                dma((2, 4, 2)),
                dma((2, 4, 2)),
                dma((2, 4, 2)),
                dma((2, 2, 2)),
                dma((2, n_shard)),
                dma((2, n_shard)),
                dma((2, 2, 2, n_shard)),
                dma((2, 2, n_shard)),
                dma((2, 2, n_shard)),
                dma((6,)),
            ],
            compiler_params=pltpu.CompilerParams(
                collective_id=0, has_side_effects=True, vmem_limit_bytes=48 * 1024 * 1024
            ),
            name="joint",
        )(vf, irf, jnp.transpose(wv, (1, 0, 2)), jnp.transpose(wi, (1, 0, 2)), tq, tk, tv, counts, mask)

    return jax.shard_map(
        shards,
        mesh=mesh,
        in_specs=(
            P("ctx", ("section", "tp")),
            P("ctx", ("section", "tp")),
            P(("section", "tp"), None, None),
            P(("section", "tp"), None, None),
            P("ctx", ("section", "tp")),
            P("ctx", ("section", "tp")),
            P("ctx", ("section", "tp")),
            P(),
            P(),
        ),
        out_specs=P("ctx", ("section", "tp")),
        check_vma=False,
    )
```

time: 628 us -> 88.3 us (0.14)
  the two profiles are of different devices: /device:TPU:493 before, /device:TPU:494 now
where the time goes in v1:
time: 88.3 us; the launch traced here: 88.1 us
  Pallas kernels  84.1 us (95%)
  local copies, waits for them, and re-layouts  3.93 us (4%)
    pallas_call x1, Pallas kernels, shards(): pl.pallas_call(functools.partial(kernel, n_section, n_ctx, n_tp), out_sha...  84.1 us
    unnamed x18, local copies, waits for them, and re-layouts  3.93 us

profile of v1, /device:TPU:494, one launch (start us, length us, event | category | flops | bytes accessed | tf_op | source)
XLA Modules:
  0.0 88.1 jit_solution(7287601566238729917)
XLA Ops:
  0.0 0.0 copy-start.6
  0.0 0.9 %copy.12.counts_ref = s32[64,2]{1,0:T(8,128)S(1)} copy(s32[64,2]{0,1:T(2,128)} %param.16) | data formatting | bytes 1024 | tf_op args[7]
  0.9 1.5 %copy.16 = bf16[96,8,768]{2,0,1:T(8,128)(2,1)S(1)} copy(bf16[96,8,768]{2,1,0:T(8,128)(2,1)} %param.12) | data formatting | bytes 2359296 | tf_op args[3]
  2.4 0.0 copy-done.6
  2.4 0.0 copy-start
  2.4 0.0 copy-start.1
  2.4 0.0 copy-start.2
  2.4 0.0 copy-start.3
  2.4 0.0 copy-start.4
  2.4 0.0 copy-start.5
  2.5 0.3 copy.15
  2.8 0.5 copy-done
  3.3 0.0 copy-done.1
  3.3 0.0 copy-done.2
  3.3 0.0 copy-done.3
  3.3 0.0 copy-done.4
  3.3 0.0 copy-done.5
  3.3 84.1 %joint.1 = bf16[256,512]{1,0:T(8,128)(2,1)S(1)} custom-call(bf16[128,128]{1,0:T(8,128)(2,1)S(1)} %copy-done.1, bf16[32,96]{1,0:T(8,128)(2,1)S(1)} %copy-done.5, bf16[8,128,768]{2,1,0:T(8,128)(2,1)S(1)} %bitcast.6, bf16[8,96,768]{2,1,0:T(8,128)(2,1)S(1)} %bitcast.7, bf16[96,512]{1,0:T(8,128)(2,1)S(1)} %copy-done, bf16[96,128]{1,0:T(8,128)(2,1)S(1)} %copy-done.3, ...), custom_call_target="tpu_custom_call" | custom-call | tf_op jit(solution)/shard_map/joint/pallas_call | solution.py:441
  87.4 0.7 copy.18
Async XLA Ops:
  0.0 2.4 %copy-start.6 = (bf16[128,8,768]{2,1,0:T(8,128)(2,1)S(1)}, bf16[128,8,768]{2,1,0:T(8,128)(2,1)}, u32[]{:S(2)}) copy-start(bf16[128,8,768]{2,1,0:T(8,128)(2,1)} %param.11) | copy-start | bytes 4718596
  2.4 0.9 %copy-start = (bf16[96,512]{1,0:T(8,128)(2,1)S(1)}, bf16[96,512]{1,0:T(8,128)(2,1)}, u32[]{:S(2)}) copy-start(bf16[96,512]{1,0:T(8,128)(2,1)} %tq_ref.1) | copy-start | bytes 294916
  2.4 0.9 %copy-start.1 = (bf16[128,128]{1,0:T(8,128)(2,1)S(1)}, bf16[128,128]{1,0:T(8,128)(2,1)}, u32[]{:S(2)}) copy-start(bf16[128,128]{1,0:T(8,128)(2,1)} %vf_ref.1) | copy-start | bytes 98308
  2.4 0.9 copy-start.2
  2.4 0.9 copy-start.3
  2.4 0.9 copy-start.4
  2.4 0.9 copy-start.5

commit v2 on v1

v2 whole, which is shorter than its diff:
```python
import functools

import jax
import jax.numpy as jnp
from jax import lax
from jax.experimental import pallas as pl
from jax.experimental.pallas import tpu as pltpu
from jax.sharding import PartitionSpec as P

HEAD_DIM = 128
D_VID = 1024
D_IR = 768
VTOK = 128
ITOK = 32
ENC = VTOK + ITOK
XTOK = 96
QPK = 4
QW = QPK * HEAD_DIM
GW = 768
KVW = 2 * HEAD_DIM
BLK = 256
PAIR = 2 * BLK

LN_EPSILON = 1e-05
NEG_LARGE = -1e30
LOG2E = 1.4426950408889634
MESH = pl.DeviceIdType.MESH

PIECES = ((ENC, XTOK), (0, ENC), (0, BLK))
TEXT, ENCODED, WHOLE = 0, 1, 2
PROJ_TICK = 4
OFFSETS = (0, PROJ_TICK)
LAG = 1


def kernel(
    n_section,
    n_ctx,
    n_tp,
    vf_ref,
    if_ref,
    w_ref,
    tq_ref,
    tk_ref,
    tv_ref,
    counts_ref,
    mask_ref,
    out_ref,
    kv,
    bias,
    feats,
    wb,
    qa,
    top,
    acc,
    kv_recv,
    own_recv,
    own_send,
    z_send,
    core_send,
    y_send,
    x_recv,
    x_send,
    w_recv,
    w_send,
    w_fwd,
    local_sem,
):
    section = lax.axis_index("section")
    ctx = lax.axis_index("ctx")
    tp = lax.axis_index("tp")
    n_z = n_ctx // 4
    half = n_z // 2
    row = ctx // (2 * n_z)
    z = (ctx // 2) % n_z
    core = ctx % 2
    shard = section * n_tp + tp
    n_shard = n_section * n_tp

    def frame_at(r, zz, k):
        return r * (2 * n_z) + zz * 2 + k

    core_peer = {"ctx": frame_at(row, z, 1 - core)}
    y_peer = {"ctx": frame_at(1 - row, z, core)}
    up = {"ctx": frame_at(row, (z + 1) % n_z, core)}
    down = {"ctx": frame_at(row, (z + n_z - 1) % n_z, core)}
    z_next = {"ctx": frame_at(row, (z + 1 + core * (n_z - 2)) % n_z, core)}
    reach = half - core
    others = [(a, b) for a in range(n_section) for b in range(n_tp) if (a, b) != (0, 0)]

    def feature_peer(a, b):
        return {"section": (section + a) % n_section, "tp": (tp + b) % n_tp}

    def weight_peer(a, b):
        peer = feature_peer(a, b)
        if b:
            peer["ctx"] = frame_at(1 - row, z, core)
        return peer

    def shard_of(a, b):
        return ((section + a) % n_section) * n_tp + (tp + b) % n_tp

    barrier = pltpu.get_barrier_semaphore()
    greeted = [core_peer, y_peer, up, down]
    greeted += [feature_peer(a, b) for a, b in others]
    greeted += [weight_peer(a, b) for a, b in others if b]
    for peer in greeted:
        pl.semaphore_signal(barrier, inc=1, device_id=peer, device_id_type=MESH)

    w_rows = w_ref.shape[1]
    w_half = w_rows // 2
    d_ir = D_IR // n_shard
    my_half = pl.ds(pl.multiple_of(core * w_half, w_half), w_half)
    locals_ = [
        pltpu.make_async_copy(vf_ref, feats.at[shard, pl.ds(0, VTOK)], local_sem.at[0]),
        pltpu.make_async_copy(tv_ref, kv.at[ctx, pl.ds(ENC, XTOK), pl.ds(HEAD_DIM, HEAD_DIM)], local_sem.at[1]),
        pltpu.make_async_copy(tk_ref, kv.at[ctx, pl.ds(ENC, XTOK), pl.ds(0, HEAD_DIM)], local_sem.at[2]),
        pltpu.make_async_copy(w_ref.at[shard, my_half], wb.at[shard, my_half], local_sem.at[3]),
    ]
    for copy in locals_:
        copy.start()
    feats[shard, VTOK:, :d_ir] = if_ref[...]

    def remote(src, dst, send_sem, recv_sem, peer):
        return pltpu.make_async_remote_copy(
            src_ref=src, dst_ref=dst, send_sem=send_sem, recv_sem=recv_sem, device_id=peer, device_id_type=MESH
        )

    def feature_send(n):
        return remote(feats.at[shard], feats.at[shard], x_send.at[n], x_recv.at[shard], feature_peer(*others[n]))

    def feature_arrival(n):
        place = feats.at[shard_of(*others[n])]
        return remote(place, place, x_send.at[n], x_recv.at[shard_of(*others[n])], core_peer)

    parts = (pl.ds(QW, KVW), pl.ds(0, QW))

    def weight_send(n, part):
        a, b = others[n]
        return remote(
            w_ref.at[shard_of(a, b), my_half, parts[part]],
            wb.at[shard, my_half, parts[part]],
            w_send.at[part, n],
            w_recv.at[part, shard],
            weight_peer(a, b),
        )

    def weight_arrival(n, part):
        src = shard_of(*others[n])
        place = wb.at[src, my_half, parts[part]]
        return remote(place, place, w_send.at[part, n], w_recv.at[part, src], core_peer)

    def weight_forward(part, k):
        place = wb.at[:, pl.ds(pl.multiple_of(k * w_half, w_half), w_half), parts[part]]
        return remote(place, place, w_fwd.at[0, part], w_fwd.at[1, part], core_peer)

    def own_swap(piece, k):
        first, count = PIECES[piece]
        place = kv.at[frame_at(row, z, k), pl.ds(first, count)]
        return remote(place, place, own_send.at[piece], own_recv.at[piece], core_peer)

    def pair_copy(r, zz, piece, sem, peer):
        first, count = PIECES[piece]
        place = kv.at[pl.ds(frame_at(r, zz, 0), 2), pl.ds(first, count)]
        return remote(place, place, sem, kv_recv.at[r * n_z + zz, piece], peer)

    def arrived(r, zz, piece):
        pair_copy(r, zz, piece, z_send.at[0, 0], core_peer).wait_recv()

    def z_of(way, distance):
        return (z + n_z + (2 * way - 1) * distance) % n_z

    def act(copy, start):
        if start:
            copy.start()
        else:
            copy.wait_send()

    def line_step(tick, piece, start):
        distance = tick - OFFSETS[piece]
        slot = tick % 2
        zz = z_of(core, distance)
        wanted = (row == 0) | ((core == 0) & (distance <= z)) | ((core == 1) & (zz < half - 1))
        goes_on = (row == 0) | (core == 1) | (z < n_z - 1)

        @pl.when((distance >= 0) & (distance <= reach) & wanted)
        def _():
            if start:
                @pl.when(distance >= 1)
                def _():
                    arrived(row, zz, piece)

            @pl.when((distance < reach) & goes_on)
            def _():
                act(pair_copy(row, zz, piece, z_send.at[piece, slot], z_next), start)

            @pl.when((row == 0) & (distance == 0) if piece == TEXT else row == 0)
            def _():
                act(pair_copy(row, zz, piece, y_send.at[piece, slot], y_peer), start)

    def text_step(tick, start):
        distance = tick - 1
        slot = tick % 2
        zz = z_of(core, distance)

        @pl.when((row == 1) & (distance >= 0) & (distance <= reach))
        def _():
            if start:
                arrived(0, zz, TEXT)

            @pl.when(distance < reach)
            def _():
                act(pair_copy(0, zz, TEXT, z_send.at[2, slot], z_next), start)

    def whole_step(tick, own, start):
        distance = tick - PROJ_TICK if own else tick - PROJ_TICK - 1
        slot = tick % 2
        zz = z_of(core, distance)
        if own:
            active = (distance >= 1) & (distance <= reach) & (zz < z)
        else:
            active = (row == 1) & (distance >= 0) & (distance <= reach)

        @pl.when(active)
        def _():
            if start and not own:
                arrived(0, zz, ENCODED)

            @pl.when(distance >= 1)
            def _():
                act(pair_copy(row if own else 0, zz, WHOLE, core_send.at[int(own), slot], core_peer), start)

    def lines(tick, start=True):
        line_step(tick, ENCODED, start)
        line_step(tick, TEXT, start)
        text_step(tick, start)

    def wholes(tick, start=True):
        whole_step(tick, True, start)
        whole_step(tick, False, start)

    def step(tick):
        lines(tick - 2, start=False)
        lines(tick)
        wholes(tick - 2, start=False)
        wholes(tick)

    def attend(first_frame, diagonal):
        rows = pl.ds(pl.multiple_of(first_frame * BLK, PAIR), PAIR)
        pair = kv[pl.ds(first_frame, 2)].reshape(PAIR, KVW)
        keys = jnp.concatenate([pair[:, :HEAD_DIM], bias[rows, :]], axis=1)
        values = jnp.concatenate([pair[:, HEAD_DIM:], jnp.ones((PAIR, HEAD_DIM), jnp.bfloat16)], axis=1)
        for h in range(QPK):
            scores = lax.dot_general(
                qa[h], keys, (((1,), (1,)), ((), ())), preferred_element_type=jnp.float32
            )
            if diagonal:
                key_slot = lax.broadcasted_iota(jnp.int32, (BLK, PAIR), 1)
                query_slot = lax.broadcasted_iota(jnp.int32, (BLK, PAIR), 0) + core * BLK
                scores = jnp.where(key_slot <= query_slot, scores, NEG_LARGE)
            old = top[h]
            new = jnp.maximum(old, jnp.max(scores, axis=1, keepdims=True))
            top[h] = new
            weights = jnp.concatenate(
                [jnp.exp2(scores[:, i : i + HEAD_DIM] - new) for i in range(0, PAIR, HEAD_DIM)], axis=1
            ).astype(jnp.bfloat16)
            factor = jnp.exp2(old - new)
            acc[h] = acc[h] * jnp.concatenate([factor, factor], axis=1) + jnp.dot(
                weights, values, preferred_element_type=jnp.float32
            )

    def first_at(turn):
        return jnp.where(turn < LAG, 2 * turn, turn + LAG)

    def compute(turn, part):
        low, high = first_at(turn), jnp.where(turn < 0, 0, first_at(turn + 1))

        def item(n, _):
            distance = low + n // 2
            way, r = part, n % 2
            zz = z_of(way, distance)
            present = (turn >= 0) & (r <= row) & (distance < high) & (distance <= half)
            if way == 1:
                present = present & (distance >= 1) & (distance < half)
            present = present & jnp.logical_not((r == row) & (distance == 0))

            @pl.when(present & ((r < row) | (zz < z)))
            def _():
                @pl.when((core != part) & (distance >= 1))
                def _():
                    arrived(r, zz, WHOLE)

                attend(frame_at(r, zz, 0), False)

            return 0

        lax.fori_loop(0, 4, item, 0)

    pl.semaphore_wait(barrier, len(greeted))
    locals_[0].wait()
    for n in range(len(others)):
        feature_send(n).start()
    locals_[1].wait()
    locals_[2].wait()
    own_swap(TEXT, core).start()
    for n in range(len(others)):
        weight_send(n, 0).start()
    own_swap(TEXT, 1 - core).wait_recv()
    lines(0)
    for n in range(len(others)):
        weight_send(n, 1).start()

    def mask_frame(f, _):
        seen = mask_ref[ctx, f]
        video_live = counts_ref[0, f] * seen
        ir_live = counts_ref[1, f] * seen
        text_live = XTOK * seen
        base = pl.multiple_of(f * BLK, BLK)
        for first, count, live in ((0, VTOK, video_live), (VTOK, ITOK, ir_live), (ENC, XTOK, text_live)):
            slot = lax.broadcasted_iota(jnp.int32, (count, HEAD_DIM), 0)
            bias[pl.ds(base + first, count), :] = jnp.where(slot < live, 0.0, NEG_LARGE).astype(jnp.bfloat16)
        return 0

    lax.fori_loop(0, n_ctx, mask_frame, 0)

    for h in range(QPK):
        lane = lax.broadcasted_iota(jnp.int32, (BLK, HEAD_DIM), 1)
        qa[h, :, HEAD_DIM:] = jnp.where(lane == 0, 1.0, 0.0).astype(jnp.bfloat16)
        top[h] = jnp.full((BLK, HEAD_DIM), NEG_LARGE, jnp.float32)
        acc[h] = jnp.zeros((BLK, 2 * HEAD_DIM), jnp.float32)

    def early(tick, _):
        step(tick)
        return 0

    lax.fori_loop(1, PROJ_TICK, early, 0)

    for n in range(len(others)):
        feature_arrival(n).wait_recv()
    for n in range(len(others)):
        feature_send(n).wait_send()

    def norm_terms(values, count):
        center = sum(jnp.sum(x, axis=1, keepdims=True) for x in values) / count
        spread = sum(jnp.sum(x * x, axis=1, keepdims=True) for x in values) / count - center * center
        return center, lax.rsqrt(spread + LN_EPSILON)

    video = [feats[n, :VTOK].astype(jnp.float32) for n in range(n_shard)]
    center, gain = norm_terms(video, D_VID)
    for n in range(n_shard):
        feats[n, :VTOK] = ((video[n] - center) * gain).astype(jnp.bfloat16)
    infra = [feats[n, VTOK:, :d_ir].astype(jnp.float32) for n in range(n_shard)]
    center, gain = norm_terms(infra, D_IR)
    for n in range(n_shard):
        feats[n, VTOK:, :d_ir] = ((infra[n] - center) * gain).astype(jnp.bfloat16)

    def take_weights(part):
        for n in range(len(others)):
            weight_arrival(n, part).wait_recv()
        weight_forward(part, core).start()
        weight_forward(part, 1 - core).wait_recv()

    def project(columns):
        d_vid = w_rows - d_ir
        rows = jnp.concatenate([feats[n, :VTOK] for n in range(n_shard)], axis=1)
        maps = jnp.concatenate([wb[n, :d_vid, columns] for n in range(n_shard)], axis=0)
        video_out = jnp.dot(rows, maps, preferred_element_type=jnp.float32)
        ir_out = sum(
            jnp.dot(feats[n, VTOK:, :d_ir], wb[n, d_vid:, columns], preferred_element_type=jnp.float32)
            for n in range(n_shard)
        )
        return video_out, ir_out

    locals_[3].wait()
    take_weights(0)
    video_out, ir_out = project(slice(QW, GW))
    kv[ctx, :VTOK, :] = video_out.astype(jnp.bfloat16)
    kv[ctx, VTOK:ENC, :] = ir_out.astype(jnp.bfloat16)
    own_swap(ENCODED, core).start()
    own_swap(ENCODED, 1 - core).wait_recv()

    lax.fori_loop(PROJ_TICK, PROJ_TICK + 2 + LAG, early, 0)

    take_weights(1)
    scale = HEAD_DIM ** (-0.5) * LOG2E
    video_out, ir_out = project(slice(0, QW))
    for h in range(QPK):
        columns = slice(h * HEAD_DIM, (h + 1) * HEAD_DIM)
        qa[h, :VTOK, :HEAD_DIM] = (video_out[:, columns] * scale).astype(jnp.bfloat16)
        qa[h, VTOK:ENC, :HEAD_DIM] = (ir_out[:, columns] * scale).astype(jnp.bfloat16)
        qa[h, ENC:, :HEAD_DIM] = (tq_ref[:, columns].astype(jnp.float32) * scale).astype(jnp.bfloat16)

    attend(frame_at(row, z, 0), True)

    def late(tick, _):
        turn = tick - PROJ_TICK - 2 - LAG
        lines(tick - 2, start=False)
        lines(tick)
        compute(turn, 0)
        wholes(tick - 2, start=False)
        wholes(tick)
        compute(turn, 1)
        return 0

    last = half + PROJ_TICK + 3
    lax.fori_loop(PROJ_TICK + 2 + LAG, last, late, 0)

    for h in range(QPK):
        out_ref[:, h * HEAD_DIM : (h + 1) * HEAD_DIM] = (
            acc[h, :, :HEAD_DIM] / acc[h, :, HEAD_DIM:]
        ).astype(jnp.bfloat16)

    for tick in (last - 2, last - 1):
        lines(tick, start=False)
        wholes(tick, start=False)
    own_swap(TEXT, core).wait_send()
    own_swap(ENCODED, core).wait_send()
    for part in range(2):
        weight_forward(part, core).wait_send()
        for n in range(len(others)):
            weight_send(n, part).wait_send()


def solution(mesh):
    n_section, n_ctx, n_tp = mesh.shape["section"], mesh.shape["ctx"], mesh.shape["tp"]
    n_shard = n_section * n_tp

    def shards(vf, irf, wv, wi, tq, tk, tv, counts, mask):
        anywhere = pl.BlockSpec(memory_space=pl.ANY)
        vmem = pl.BlockSpec(memory_space=pltpu.VMEM)
        smem = pl.BlockSpec(memory_space=pltpu.SMEM)
        dma = pltpu.SemaphoreType.DMA
        adapters = jnp.concatenate([jnp.transpose(wv, (1, 0, 2)), jnp.transpose(wi, (1, 0, 2))], axis=1)
        return pl.pallas_call(
            functools.partial(kernel, n_section, n_ctx, n_tp),
            out_shape=jax.ShapeDtypeStruct((BLK, QW), jnp.bfloat16),
            in_specs=[anywhere, vmem, anywhere, vmem] + [anywhere] * 2 + [smem] * 2,
            out_specs=vmem,
            scratch_shapes=[
                pltpu.VMEM((n_ctx, BLK, KVW), jnp.bfloat16),
                pltpu.VMEM((n_ctx * BLK, HEAD_DIM), jnp.bfloat16),
                pltpu.VMEM((n_shard, ENC, D_VID // n_shard), jnp.bfloat16),
                pltpu.VMEM((n_shard, (D_VID + D_IR) // n_shard, GW), jnp.bfloat16),
                pltpu.VMEM((QPK, BLK, 2 * HEAD_DIM), jnp.bfloat16),
                pltpu.VMEM((QPK, BLK, HEAD_DIM), jnp.float32),
                pltpu.VMEM((QPK, BLK, 2 * HEAD_DIM), jnp.float32),
                dma((n_ctx // 2, 3)),
                dma((2,)),
                dma((2,)),
                dma((3, 2)),
                dma((2, 2)),
                dma((2, 2)),
                dma((n_shard,)),
                dma((n_shard,)),
                dma((2, n_shard)),
                dma((2, n_shard)),
                dma((2, 2)),
                dma((4,)),
            ],
            compiler_params=pltpu.CompilerParams(
                collective_id=0, has_side_effects=True, vmem_limit_bytes=48 * 1024 * 1024
            ),
            name="joint",
        )(vf, irf, adapters, tq, tk, tv, jnp.transpose(counts), mask)

    return jax.shard_map(
        shards,
        mesh=mesh,
        in_specs=(
            P("ctx", ("section", "tp")),
            P("ctx", ("section", "tp")),
            P(("section", "tp"), None, None),
            P(("section", "tp"), None, None),
            P("ctx", ("section", "tp")),
            P("ctx", ("section", "tp")),
            P("ctx", ("section", "tp")),
            P(),
            P(),
        ),
        out_specs=P("ctx", ("section", "tp")),
        check_vma=False,
    )
```

time: 88.3 us -> 82.4 us (0.933)
  the two profiles are of different devices: /device:TPU:494 before, /device:TPU:489 now
where the time goes in v2:
time: 82.4 us; the launch traced here: 82.3 us
  Pallas kernels  78.6 us (95%)
  local copies, waits for them, and re-layouts  3.42 us (4%)
    pallas_call x1, Pallas kernels, shards(): pl.pallas_call(functools.partial(kernel, n_section, n_ctx, n_tp), out_sha...  78.6 us
    unnamed x19, local copies, waits for them, and re-layouts  3.42 us

profile of v2, /device:TPU:489, one launch (start us, length us, event | category | flops | bytes accessed | tf_op | source)
XLA Modules:
  0.0 82.3 jit_solution(13048717298239270428)
XLA Ops:
  0.0 0.0 copy-start.7
  0.0 1.6 %copy.15 = bf16[96,8,768]{2,0,1:T(8,128)(2,1)S(1)} copy(bf16[96,8,768]{2,1,0:T(8,128)(2,1)} %param.12) | data formatting | bytes 2359296 | tf_op args[3]
  1.6 0.2 copy-done.7
  1.8 0.3 copy.14
  2.1 0.0 copy-start
  2.1 0.0 copy-start.1
  2.1 0.0 copy-start.2
  2.1 0.0 copy-start.3
  2.1 0.0 copy-start.4
  2.1 0.0 copy-start.5
  2.1 0.0 copy-start.6
  2.1 0.2 pad_maximum_fusion.w_ref
  2.3 0.6 copy-done
  3.0 0.0 copy-done.1
  3.0 0.0 copy-done.2
  3.0 0.0 copy-done.3
  3.0 0.0 copy-done.4
  3.0 0.0 copy-done.5
  3.0 0.0 copy-done.6
  3.0 78.6 %joint.1 = bf16[256,512]{1,0:T(8,128)(2,1)S(1)} custom-call(bf16[128,128]{1,0:T(8,128)(2,1)S(1)} %copy-done.1, bf16[32,96]{1,0:T(8,128)(2,1)S(1)} %copy-done.5, bf16[8,224,768]{2,1,0:T(8,128)(2,1)S(1)} %pad_maximum_fusion.w_ref, bf16[96,512]{1,0:T(8,128)(2,1)S(1)} %copy-done, bf16[96,128]{1,0:T(8,128)(2,1)S(1)} %copy-done.3, bf16[96,128]{1,0:T(8,128)(2,1)S(1)} %copy-done.4, ...), custom_call_target="tpu_custom_call" | custom-call | tf_op jit(solution)/shard_map/joint/pallas_call | solution.py:434
  81.6 0.7 copy.17
Async XLA Ops:
  0.0 1.8 %copy-start.7 = (bf16[128,8,768]{2,1,0:T(8,128)(2,1)S(1)}, bf16[128,8,768]{2,1,0:T(8,128)(2,1)}, u32[]{:S(2)}) copy-start(bf16[128,8,768]{2,1,0:T(8,128)(2,1)} %param.11) | copy-start | bytes 4718596
  2.1 0.9 %copy-start = (bf16[96,512]{1,0:T(8,128)(2,1)S(1)}, bf16[96,512]{1,0:T(8,128)(2,1)}, u32[]{:S(2)}) copy-start(bf16[96,512]{1,0:T(8,128)(2,1)} %tq_ref.1) | copy-start | bytes 294916
  2.1 0.9 %copy-start.1 = (bf16[128,128]{1,0:T(8,128)(2,1)S(1)}, bf16[128,128]{1,0:T(8,128)(2,1)}, u32[]{:S(2)}) copy-start(bf16[128,128]{1,0:T(8,128)(2,1)} %vf_ref.1) | copy-start | bytes 98308
  2.1 0.9 %copy-start.2 = (s32[64,64]{1,0:T(8,128)S(1)}, s32[64,64]{1,0:T(8,128)}, u32[]{:S(2)}) copy-start(s32[64,64]{1,0:T(8,128)} %mask_ref.1) | copy-start | bytes 49156
  2.1 0.9 %copy-start.3 = (bf16[96,128]{1,0:T(8,128)(2,1)S(1)}, bf16[96,128]{1,0:T(8,128)(2,1)}, u32[]{:S(2)}) copy-start(bf16[96,128]{1,0:T(8,128)(2,1)} %tk_ref.1) | copy-start | bytes 73732
  2.1 0.9 %copy-start.4 = (bf16[96,128]{1,0:T(8,128)(2,1)S(1)}, bf16[96,128]{1,0:T(8,128)(2,1)}, u32[]{:S(2)}) copy-start(bf16[96,128]{1,0:T(8,128)(2,1)} %tv_ref.1) | copy-start | bytes 73732
  2.1 0.9 %copy-start.5 = (bf16[32,96]{1,0:T(8,128)(2,1)S(1)}, bf16[32,96]{1,0:T(8,128)(2,1)}, u32[]{:S(2)}) copy-start(bf16[32,96]{1,0:T(8,128)(2,1)} %if_ref.1) | copy-start | bytes 18436
  2.1 0.8 %copy-start.6 = (s32[64,2]{0,1:T(2,128)S(1)}, s32[64,2]{0,1:T(2,128)}, u32[]{:S(2)}) copy-start(s32[64,2]{0,1:T(2,128)} %param.16) | copy-start | bytes 1540
